TPU v7x, 32 devices: a whole 2x2x4 slice. The times are simulated.
32 devices in a mesh: row: 4 (over z), col: 8 (over y, x, core).
Axes of the slice: x: 2, y: 2, z: 4, core: 2. Of those that a mesh axis runs over, the one named last changes fastest.
Arguments:
- kernel: bfloat16 [16384, 16384], P('row', 'col'), may hold values from -6 to 6
- labels: int32 [3, 16384], replicated, may hold values from 0 to 63, as said below
Outputs:
- distance: float32 [3, 16384, 64], P(None, ('row', 'col'))
- objective: float32 [3], replicated
Inputs may be any that keep to these rules, and one draw needn't show every extreme that they name: `labels`: in every iteration every cluster of 0 to 63 is named by at least one series.
All inputs are finite; a program needn't handle non-finite values.
Results may differ from a plain program's by a relative error of at most 0.0003.
Values sent between devices are 32-bit elements; how exact they have to be, the bound alone decides.
A program may use at most 64 MiB of HBM per device.

v0:
```python
import jax
import jax.numpy as jnp
from jax import lax
from jax.sharding import PartitionSpec as P

SERIES = 16384
CLUSTERS = 64
ITERS = 3


def shards(kernel, labels):
    rows_block, cols_block = kernel.shape
    slice_rows = rows_block // lax.axis_size("col")
    row_base = lax.axis_index("row") * rows_block
    col_base = lax.axis_index("col") * cols_block
    my_offset = lax.axis_index("col") * slice_rows
    clusters = jnp.arange(CLUSTERS, dtype=jnp.int32)
    col_labels = lax.dynamic_slice_in_dim(labels, col_base, cols_block, 1)
    block_labels = lax.dynamic_slice_in_dim(labels, row_base, rows_block, 1)
    counts = jnp.sum((labels[:, :, None] == clusters).astype(jnp.float32), axis=1)

    def encode(chosen):
        flat = chosen.T[:, :, None] == clusters[None, None, :]
        return flat.reshape(chosen.shape[1], -1).astype(jnp.bfloat16)

    local = jnp.dot(kernel, encode(col_labels), preferred_element_type=jnp.float32)
    whole = lax.psum(local, "col")
    totals = lax.psum(jnp.sum(encode(block_labels).astype(jnp.float32) * whole, axis=0), "row")
    sums = lax.dynamic_slice_in_dim(whole, my_offset, slice_rows, 0)
    sums, totals = (sums, totals)
    sums = sums.reshape(slice_rows, ITERS, CLUSTERS).transpose(1, 0, 2)
    totals = totals.reshape(ITERS, CLUSTERS)
    distance = -2.0 * sums / counts[:, None, :] + totals[:, None, :] / (counts * counts)[:, None, :]
    objective = 1.0 - jnp.sum(totals / counts, axis=1) / SERIES
    return (distance, objective)


def solution(mesh):
    return jax.shard_map(
        shards,
        mesh=mesh,
        in_specs=(P("row", "col"), P()),
        out_specs=(P(None, ("row", "col"), None), P()),
        check_vma=False,
    )
```

profile of v0, /device:TPU:0, one launch (start us, length us, event | category | flops | bytes accessed | tf_op | source)
XLA Modules:
  0.0 117.1 jit_solution(2459755366757021118)
XLA Ops:
  7.2 0.0 all-reduce.2.cloned.1.call-start
  7.2 0.1 eq.56
  7.3 0.8 dynamic-slice_bitcast_fusion.1
  8.1 0.3 bitcast_compare_fusion.1
  8.4 13.0 %convolution_bitcast_fusion = f32[4096,192]{0,1:T(8,128)} fusion(pred[2048,192]{0,1:T(32,128)(4,1)S(1)} %bitcast_compare_fusion.1, bf16[4096,2048]{1,0:T(8,128)(2,1)} %param.2), kind=kOutput, calls=%fused_computation.2 | convolution fusion | flops 3221225472 | bytes 20316160 | tf_op jit(solution)/shard_map/dot_general | solution.py:26
  21.4 0.0 copy-start
  21.4 0.0 all-reduce.2.cloned.1.call-update
  21.4 0.9 copy-done
  22.4 0.5 bitcast_compare_fusion
  22.9 2.0 %convert_reduce_fusion = f32[3,64]{1,0:T(4,128)S(1)} fusion(s32[3,16384]{1,0:T(4,128)S(1)} %copy-done), kind=kLoop, calls=%fused_computation | loop fusion | flops 9436992 | bytes 197376 | tf_op jit(solution)/shard_map/reduce_sum | solution.py:20
  24.9 68.7 %all-reduce.2.cloned.1.call-done = f32[4096,192]{0,1:T(8,128)} async-done(((f32[4096,192]{0,1:T(8,128)}), f32[4096,192]{0,1:T(8,128)}) %all-reduce.2.cloned.1.call-update) | async-done | bytes 3145744 | tf_op jit(solution)/shard_map/psum | solution.py:27
  93.6 2.4 %multiply_reduce_fusion = f32[192]{0:T(256)S(1)} fusion(f32[4096,192]{0,1:T(8,128)} %all-reduce.2.cloned.1.call-done, pred[4096,192]{0,1:T(8,128)(4,1)S(1)} %bitcast_compare_fusion), kind=kLoop, calls=%fused_computation.4 | loop fusion | flops 3145536 | bytes 3932928 | tf_op jit(solution)/shard_map/reduce_sum | solution.py:28
  96.0 0.1 broadcast_in_dim_reshape.3
  96.1 11.7 %psum.15 = f32[3,64]{1,0:T(4,128)S(1)} all-reduce(f32[3,64]{1,0:T(4,128)S(1)} %broadcast_in_dim_reshape.3), channel_id=1, replica_groups=mesh['row'=4,'col'=8] {'row'}, use_global_device_ids=true, to_apply=%region_3.0 | all-reduce | flops 192 | bytes 1536 | tf_op jit(solution)/shard_map/psum | solution.py:28
  107.8 0.1 divide_reduce_fusion
  107.9 0.5 multiply_subtract_fusion
  108.4 1.0 dynamic-slice_multiply_fusion
  109.4 0.9 add_bitcast_fusion
  (2 shorter events, 0.0 us)
Async XLA Ops:
  7.2 86.4 %all-reduce.2.cloned.1.call-start = ((), (), s32[]{:S(2)}) async-start(), calls=%async_computation | async-start | bytes 6291456 | tf_op jit(solution)/shard_map/psum | solution.py:27
  21.4 0.9 copy-start
Sparse Core Ops, SparseCore 0:
  21.6 71.9 all-reduce.1
where the time goes:
time: 117 us
  waiting for transfers between devices  68.8 us (59%)
  between operations  14.1 us (12%)
  matrix products  13 us (11%)
  blocking collectives  11.7 us (10%)
  other arithmetic  7.7 us (7%)
  local copies, waits for them, and re-layouts  1.86 us (2%)
    psum x1, waiting for transfers between devices, shards(): whole = lax.psum(local, 'col')  68.7 us
    dot_general x1, matrix products, shards(): jnp.dot(kernel, encode(col_labels), preferred_element_type=jnp.float32)  13 us
    psum x1, blocking collectives, shards(): lax.psum(jnp.sum(encode(block_labels).astype(jnp.float32) * whole, axis=0...  11.7 us
    reduce_sum x1, other arithmetic, shards(): jnp.sum(encode(block_labels).astype(jnp.float32) * whole, axis=0)  2.41 us
  transfers between devices with their start and end apart: 1, of which 1 were waited for; matrix products, arithmetic and copies ran while one was open for 2% of the time, Pallas kernels for 0%

commit v1 on v0

--- a/solution.py
+++ b/solution.py
@@ -24,7 +24,9 @@
         return flat.reshape(chosen.shape[1], -1).astype(jnp.bfloat16)
 
     local = jnp.dot(kernel, encode(col_labels), preferred_element_type=jnp.float32)
-    whole = lax.psum(local, "col")
+    whole = local
+    for hop in (1, 2, 4):
+        whole = whole + lax.ppermute(whole, "col", [(dev, dev ^ hop) for dev in range(8)])
     totals = lax.psum(jnp.sum(encode(block_labels).astype(jnp.float32) * whole, axis=0), "row")
     sums = lax.dynamic_slice_in_dim(whole, my_offset, slice_rows, 0)
     sums, totals = (sums, totals)

time: 117 us -> 178 us (1.52)
  waiting for transfers between devices: 68.8 us -> 138 us
  between operations: 14.1 us -> 0.68 us
  starting transfers between devices: 0.04 us -> 5.3 us
  matrix products: 13 us -> 9.14 us
  other arithmetic: 7.7 us -> 11.3 us
    ppermute x0 -> x3, waiting for transfers between devices: none -> 138 us  [shards(): lax.ppermute(whole, 'col', [(dev, dev ^ hop) for dev in range(8)])]
    psum x1 -> x0, waiting for transfers between devices: 68.7 us -> none  [shards(): whole = lax.psum(local, 'col')]
    ppermute x0 -> x3, starting transfers between devices: none -> 5.3 us  [shards(): lax.ppermute(whole, 'col', [(dev, dev ^ hop) for dev in range(8)])]
    dot_general x1, matrix products: 13 us -> 9.14 us  [shards(): jnp.dot(kernel, encode(col_labels), preferred_element_type=jnp.float32)]
    reduce_sum x1, other arithmetic: 2.41 us -> 4.43 us  [shards(): jnp.sum(encode(block_labels).astype(jnp.float32) * whole, axis=0)]
  transfers between devices with their start and end apart: 1 -> 3, of which waited for: 1 -> 3; matrix products, arithmetic and copies ran while one was open for 2% -> 2% of each run, Pallas kernels for 0% -> 0%
where the time goes in v1:
time: 178 us; the launch traced here: 177 us
  waiting for transfers between devices  138 us (78%)
  blocking collectives  11.9 us (7%)
  other arithmetic  11.3 us (6%)
  matrix products  9.14 us (5%)
  starting transfers between devices  5.3 us (3%)
    ppermute x3, waiting for transfers between devices, shards(): lax.ppermute(whole, 'col', [(dev, dev ^ hop) for dev in range(8)])  138 us
    psum x1, blocking collectives, shards(): lax.psum(jnp.sum(encode(block_labels).astype(jnp.float32) * whole, axis=0...  11.9 us
    dot_general x1, matrix products, shards(): jnp.dot(kernel, encode(col_labels), preferred_element_type=jnp.float32)  9.14 us
    ppermute x3, starting transfers between devices, shards(): lax.ppermute(whole, 'col', [(dev, dev ^ hop) for dev in range(8)])  5.3 us
    reduce_sum x1, other arithmetic, shards(): jnp.sum(encode(block_labels).astype(jnp.float32) * whole, axis=0)  4.43 us
  transfers between devices with their start and end apart: 3, of which 3 were waited for; matrix products, arithmetic and copies ran while one was open for 2% of the time, Pallas kernels for 0%

profile of v1, /device:TPU:0, one launch (start us, length us, event | category | flops | bytes accessed | tf_op | source)
XLA Modules:
  0.0 177.5 jit_solution(6028146422009010286)
XLA Ops:
  0.6 0.1 eq.56
  0.7 0.8 dynamic-slice_bitcast_fusion.1
  1.5 0.3 bitcast_compare_fusion.1
  1.8 9.1 %convolution_bitcast_fusion = f32[4096,192]{0,1:T(8,128)S(1)} fusion(pred[2048,192]{0,1:T(32,128)(4,1)S(1)} %bitcast_compare_fusion.1, bf16[4096,2048]{1,0:T(8,128)(2,1)} %param.2), kind=kOutput, calls=%fused_computation.2 | convolution fusion | flops 3221225472 | bytes 20316160 | tf_op jit(solution)/shard_map/dot_general | solution.py:26
  10.9 0.6 collective-permute-start
  11.5 5.3 %collective-permute-done = f32[4096,192]{0,1:T(8,128)S(1)} collective-permute-done((f32[4096,192]{0,1:T(8,128)S(1)}, f32[4096,192]{0,1:T(8,128)S(1)}, u32[]{:S(2)}, u32[]{:S(2)}) %collective-permute-start) | collective-permute-done | bytes 3145760 | tf_op jit(solution)/shard_map/ppermute | solution.py:29
  16.8 0.3 add.32
  17.1 0.0 copy-start
  17.1 2.9 %collective-permute-start.1 = (f32[4096,192]{0,1:T(8,128)S(1)}, f32[4096,192]{0,1:T(8,128)S(1)}, u32[]{:S(2)}, u32[]{:S(2)}) collective-permute-start(f32[4096,192]{0,1:T(8,128)S(1)} %add.32), channel_id=1, source_target_pairs={{0,2},{1,3},{2,0},{3,1},{4,6},{5,7},{6,4},{7,5},{8,10},{9,11},{10,... | collective-permute-start | bytes 9437192 | tf_op jit(solution)/shard_map/ppermute | solution.py:29
  20.0 68.4 %collective-permute-done.1 = f32[4096,192]{0,1:T(8,128)S(1)} collective-permute-done((f32[4096,192]{0,1:T(8,128)S(1)}, f32[4096,192]{0,1:T(8,128)S(1)}, u32[]{:S(2)}, u32[]{:S(2)}) %collective-permute-start.1) | collective-permute-done | bytes 3145760 | tf_op jit(solution)/shard_map/ppermute | solution.py:29
  88.4 0.3 add.33
  88.8 1.8 %collective-permute-start.2 = (f32[4096,192]{0,1:T(8,128)S(1)}, f32[4096,192]{0,1:T(8,128)}, u32[]{:S(2)}, u32[]{:S(2)}) collective-permute-start(f32[4096,192]{0,1:T(8,128)S(1)} %add.33), channel_id=1, source_target_pairs={{0,4},{1,5},{2,6},{3,7},{4,0},{5,1},{6,2},{7,3},{8,12},{9,13},{10,... | collective-permute-start | bytes 9437192 | tf_op jit(solution)/shard_map/ppermute | solution.py:29
  90.6 0.0 copy-done
  90.6 1.4 bitcast_compare_fusion
  92.0 2.0 %convert_reduce_fusion = f32[3,64]{1,0:T(4,128)S(1)} fusion(s32[3,16384]{1,0:T(4,128)S(1)} %copy-done), kind=kLoop, calls=%fused_computation | loop fusion | flops 9436992 | bytes 197376 | tf_op jit(solution)/shard_map/reduce_sum | solution.py:20
  94.0 64.5 %collective-permute-done.2 = f32[4096,192]{0,1:T(8,128)} collective-permute-done((f32[4096,192]{0,1:T(8,128)S(1)}, f32[4096,192]{0,1:T(8,128)}, u32[]{:S(2)}, u32[]{:S(2)}) %collective-permute-start.2) | collective-permute-done | bytes 3145760 | tf_op jit(solution)/shard_map/ppermute | solution.py:29
  158.5 4.4 %multiply_reduce_fusion = (f32[192]{0:T(256)S(1)}, f32[4096,192]{0,1:T(8,128)}) fusion(pred[4096,192]{0,1:T(8,128)(4,1)} %bitcast_compare_fusion, f32[4096,192]{0,1:T(8,128)S(1)} %add.33, f32[4096,192]{0,1:T(8,128)} %collective-permute-done.2), kind=kLoop, calls=%fused_computation.4 | loop fusion | flops 3931968 | bytes 10224384 | tf_op jit(solution)/shard_map/reduce_sum | solution.py:30
  162.9 0.1 broadcast_in_dim_reshape.3
  163.0 11.9 %psum.7 = f32[3,64]{1,0:T(4,128)S(1)} all-reduce(f32[3,64]{1,0:T(4,128)S(1)} %broadcast_in_dim_reshape.3), channel_id=1, replica_groups=mesh['row'=4,'col'=8] {'row'}, use_global_device_ids=true, to_apply=%region_2.0 | all-reduce | flops 192 | bytes 1536 | tf_op jit(solution)/shard_map/psum | solution.py:30
  174.9 0.1 divide_reduce_fusion
  175.1 0.5 multiply_subtract_fusion
  175.6 1.0 dynamic-slice_multiply_fusion
  176.6 0.9 add_bitcast_fusion
  (2 shorter events, 0.0 us)
Async XLA Ops:
  10.9 5.8 %collective-permute-start = (f32[4096,192]{0,1:T(8,128)S(1)}, f32[4096,192]{0,1:T(8,128)S(1)}, u32[]{:S(2)}, u32[]{:S(2)}) collective-permute-start(f32[4096,192]{0,1:T(8,128)S(1)} %convolution_bitcast_fusion), channel_id=1, source_target_pairs={{0,1},{1,0},{2,3},{3,2},{4,5},{5,4},{6,7},{7,6},{8,9},{9,8},{10,11... | collective-permute-start | bytes 9437192 | tf_op jit(solution)/shard_map/ppermute | solution.py:29
  17.1 73.5 %copy-start = (s32[3,16384]{1,0:T(4,128)S(1)}, s32[3,16384]{1,0:T(4,128)}, u32[]{:S(2)}) copy-start(s32[3,16384]{1,0:T(4,128)} %param.3) | copy-start | bytes 589828
  17.1 71.3 %collective-permute-start.1 = (f32[4096,192]{0,1:T(8,128)S(1)}, f32[4096,192]{0,1:T(8,128)S(1)}, u32[]{:S(2)}, u32[]{:S(2)}) collective-permute-start(f32[4096,192]{0,1:T(8,128)S(1)} %add.32), channel_id=1, source_target_pairs={{0,2},{1,3},{2,0},{3,1},{4,6},{5,7},{6,4},{7,5},{8,10},{9,11},{10,... | collective-permute-start | bytes 9437192 | tf_op jit(solution)/shard_map/ppermute | solution.py:29
  88.8 69.7 %collective-permute-start.2 = (f32[4096,192]{0,1:T(8,128)S(1)}, f32[4096,192]{0,1:T(8,128)}, u32[]{:S(2)}, u32[]{:S(2)}) collective-permute-start(f32[4096,192]{0,1:T(8,128)S(1)} %add.33), channel_id=1, source_target_pairs={{0,4},{1,5},{2,6},{3,7},{4,0},{5,1},{6,2},{7,3},{8,12},{9,13},{10,... | collective-permute-start | bytes 9437192 | tf_op jit(solution)/shard_map/ppermute | solution.py:29
